TPU v7x, 32 devices: a whole 2x2x4 slice. The times are simulated.
32 devices in a mesh: tok: 4 (over z), head: 8 (over y, x, core).
Axes of the slice: x: 2, y: 2, z: 4, core: 2. Of those that a mesh axis runs over, the one named last changes fastest.
Arguments:
- block_input: bfloat16 [4, 1536, 2048], P('tok', 'head'), may hold values from -6 to 6
- segment_ids: int32 [4, 1536], P('tok'), may hold values from 0 to 3, as said below
- positions: int32 [4, 1536], P('tok'), may hold values from 0 to 1023, as said below
- attention_gain: float32 [2048], replicated, may hold values from 0.5 to 1.5
- query_down: bfloat16 [2048, 1024], replicated, may hold values from -0.125 to 0.125
- query_gain: float32 [1024], replicated, may hold values from 0.5 to 1.5
- query_up: bfloat16 [1024, 4096], P(None, 'head'), may hold values from -0.1875 to 0.1875
- key_proj: bfloat16 [2048, 256], replicated, may hold values from -0.125 to 0.125
- value_proj: bfloat16 [2048, 256], replicated, may hold values from -0.125 to 0.125
- out_proj: bfloat16 [4096, 2048], P('head'), may hold values from -0.375 to 0.375
- feed_gain: float32 [2048], replicated, may hold values from 0.5 to 1.5
- gate_weight: bfloat16 [2048, 5632], P(None, 'head'), may hold values from -0.125 to 0.125
- up_weight: bfloat16 [2048, 5632], P(None, 'head'), may hold values from -0.125 to 0.125
- down_weight: bfloat16 [5632, 2048], P('head'), may hold values from -0.078125 to 0.078125
- out_grad: bfloat16 [4, 1536, 2048], P('tok', 'head'), may hold values from -6 to 6
Outputs:
- block_output: bfloat16 [4, 1536, 2048], P('tok', 'head')
- input_gradient: float32 [4, 1536, 2048], P('tok', 'head')
- attention_gain_gradient: float32 [2048], replicated
- query_down_gradient: float32 [2048, 1024], replicated
- query_gain_gradient: float32 [1024], replicated
- query_up_gradient: float32 [1024, 4096], P(None, 'head')
- key_proj_gradient: float32 [2048, 256], replicated
- value_proj_gradient: float32 [2048, 256], replicated
- out_proj_gradient: float32 [4096, 2048], P('head')
- feed_gain_gradient: float32 [2048], replicated
- gate_weight_gradient: float32 [2048, 5632], P(None, 'head')
- up_weight_gradient: float32 [2048, 5632], P(None, 'head')
- down_weight_gradient: float32 [5632, 2048], P('head')
Inputs may be any that keep to these rules, and one draw needn't show every extreme that they name: `segment_ids`: within each pack the ids start at 0 and never fall; the first document of every pack has min(1536, max(1024, 768)) tokens, and every pack has the same number of documents. Within a document the positions rise by one from token to token; the first document of every pack starts at 0.
All inputs are finite; a program needn't handle non-finite values.
Results may differ from a plain program's by a relative error of at most 0.023.
Values may be sent and summed in bfloat16 or wider, within the bound.
No kernel may reach another device: no remote copies, remote signals or barrier semaphores. Data moves between devices by JAX's collectives and lax.ppermute only.
A program may use at most 256 MiB of HBM per device.

v0:
```python
import math
import jax
import jax.numpy as jnp
from jax import lax
from jax.sharding import PartitionSpec as P

norm_epsilon = 1e-05
rope_base = 10000.0


def normalize(value, gain):
    scale = lax.rsqrt(jnp.mean(value * value, axis=-1, keepdims=True) + norm_epsilon)
    return value * scale * gain


def norm_backward(value, gain, upper):
    scale = lax.rsqrt(jnp.mean(value * value, axis=-1, keepdims=True) + norm_epsilon)
    scaled = upper * gain
    lower = scale * scaled - value * (scale * scale * scale) * jnp.mean(
        scaled * value, axis=-1, keepdims=True
    )
    return (lower, jnp.sum(upper * value * scale, axis=0))


def rotation(places, head_width):
    half = head_width // 2
    steps = jnp.arange(half).astype(jnp.float32) * (2.0 / head_width)
    inverse = jnp.exp(steps * -math.log(rope_base))
    angles = places.astype(jnp.float32)[:, None] * inverse[None, :]
    return (jnp.cos(angles), jnp.sin(angles))


def rotate(value, cosine, sine):
    half = value.shape[-1] // 2
    first = value[..., :half]
    second = value[..., half:]
    return jnp.concatenate(
        [first * cosine - second * sine, second * cosine + first * sine], axis=-1
    )


def right_transposed(left, right):
    return lax.dot_general(
        left, right, (((1,), (1,)), ((), ())), preferred_element_type=jnp.float32
    )


def left_transposed(left, right):
    return lax.dot_general(
        left, right, (((0,), (0,)), ((), ())), preferred_element_type=jnp.float32
    )


def allowed_block(segments, start, block, key_order):
    query_order = start + jnp.arange(block)
    own_segments = lax.dynamic_slice_in_dim(segments, start, block, 0)
    return (key_order[None, :] <= query_order[:, None]) & (
        segments[None, :] == own_segments[:, None]
    )


def block_scores(queries, keys, segments, start, block, key_order, scale):
    query_block = lax.dynamic_slice_in_dim(queries, start, block, 0)
    scores = (
        jnp.einsum("bhd,kd->hbk", query_block, keys, preferred_element_type=jnp.float32) * scale
    )
    allowed = allowed_block(segments, start, block, key_order)
    return (query_block, jnp.where(allowed[None], scores, -1e30))


def attend_forward(queries, keys, values, segments, block, scale):
    length = queries.shape[0]
    key_order = jnp.arange(length)

    def one_block(index):
        query_block, scores = block_scores(
            queries, keys, segments, index * block, block, key_order, scale
        )
        top = jnp.max(scores, axis=-1, keepdims=True)
        weights = jnp.exp(scores - top)
        total = jnp.sum(weights, axis=-1, keepdims=True)
        probs = (weights / total).astype(jnp.bfloat16)
        result = jnp.einsum("hbk,kd->bhd", probs, values, preferred_element_type=jnp.float32)
        return (result.astype(jnp.bfloat16), (top + jnp.log(total))[..., 0])

    outputs, log_totals = lax.map(one_block, jnp.arange(length // block))
    return (outputs.reshape(length, -1), log_totals)


def attend_backward(queries, keys, values, segments, log_totals, outer_grad, block, scale):
    length = queries.shape[0]
    key_order = jnp.arange(length)

    def one_block(carry, index):
        keys_total, values_total = carry
        start = index * block
        query_block, scores = block_scores(queries, keys, segments, start, block, key_order, scale)
        grad_block = lax.dynamic_slice_in_dim(outer_grad, start, block, 0)
        probs = jnp.exp(scores - log_totals[index][..., None])
        prob_grad = jnp.einsum(
            "bhd,kd->hbk", grad_block, values, preferred_element_type=jnp.float32
        )
        centre = jnp.sum(probs * prob_grad, axis=-1, keepdims=True)
        score_grad = (probs * (prob_grad - centre)).astype(jnp.bfloat16)
        query_grad = (
            jnp.einsum("hbk,kd->bhd", score_grad, keys, preferred_element_type=jnp.float32) * scale
        )
        keys_total = (
            keys_total
            + jnp.einsum("hbk,bhd->kd", score_grad, query_block, preferred_element_type=jnp.float32)
            * scale
        )
        values_total = values_total + jnp.einsum(
            "hbk,bhd->kd",
            probs.astype(jnp.bfloat16),
            grad_block,
            preferred_element_type=jnp.float32,
        )
        return ((keys_total, values_total), query_grad)

    initial = (jnp.zeros(keys.shape, jnp.float32), jnp.zeros(values.shape, jnp.float32))
    (keys_total, values_total), query_grads = lax.scan(
        one_block, initial, jnp.arange(length // block)
    )
    return (query_grads.reshape(queries.shape), keys_total, values_total)


def body(
    block_input,
    segment_ids,
    positions,
    attention_gain,
    query_down,
    query_gain,
    query_up,
    key_proj,
    value_proj,
    out_proj,
    feed_gain,
    gate_weight,
    up_weight,
    down_weight,
    out_grad,
):
    rows = block_input.shape[1]
    segments = segment_ids[0]
    places = positions[0]
    length = segments.shape[0]
    head_width = key_proj.shape[1]
    heads_here = query_up.shape[1] // head_width
    block = min(512, length)
    scale = 1.0 / math.sqrt(head_width)
    first_row = lax.axis_index("head") * rows
    rows_in = block_input[0].astype(jnp.float32)
    normed_rows = normalize(rows_in, attention_gain).astype(jnp.bfloat16)
    normed_in = lax.all_gather(normed_rows, "head", axis=0, tiled=True)
    latent = jnp.dot(normed_in, query_down, preferred_element_type=jnp.float32)
    latent_normed = normalize(latent, query_gain).astype(jnp.bfloat16)
    cosine, sine = rotation(places, head_width)
    query_pre = jnp.dot(latent_normed, query_up, preferred_element_type=jnp.float32).reshape(
        length, heads_here, head_width
    )
    queries = rotate(query_pre, cosine[:, None], sine[:, None]).astype(jnp.bfloat16)
    keys = rotate(
        jnp.dot(normed_in, key_proj, preferred_element_type=jnp.float32), cosine, sine
    ).astype(jnp.bfloat16)
    values = jnp.dot(normed_in, value_proj, preferred_element_type=jnp.float32).astype(jnp.bfloat16)
    mixed, log_totals = attend_forward(queries, keys, values, segments, block, scale)
    attention = lax.psum_scatter(
        jnp.dot(mixed, out_proj, preferred_element_type=jnp.float32).astype(jnp.bfloat16),
        "head",
        scatter_dimension=0,
        tiled=True,
    ).astype(jnp.float32)
    middle = rows_in + attention
    normed_mid_rows = normalize(middle, feed_gain).astype(jnp.bfloat16)
    normed_mid = lax.all_gather(normed_mid_rows, "head", axis=0, tiled=True)
    gate = jnp.dot(normed_mid, gate_weight, preferred_element_type=jnp.float32)
    upward = jnp.dot(normed_mid, up_weight, preferred_element_type=jnp.float32)
    sigmoid_gate = jax.nn.sigmoid(gate)
    swish = gate * sigmoid_gate
    hidden = (swish * upward).astype(jnp.bfloat16)
    feed_rows = lax.psum_scatter(
        jnp.dot(hidden, down_weight, preferred_element_type=jnp.float32).astype(jnp.bfloat16),
        "head",
        scatter_dimension=0,
        tiled=True,
    ).astype(jnp.float32)
    block_output = (middle + feed_rows).astype(jnp.bfloat16)
    cotangent_rows = out_grad[0]
    cotangent = lax.all_gather(cotangent_rows, "head", axis=0, tiled=True)
    hidden_grad = right_transposed(cotangent, down_weight)
    down_gradient = left_transposed(hidden, cotangent)
    gate_grad = (hidden_grad * upward * sigmoid_gate * (1.0 + gate * (1.0 - sigmoid_gate))).astype(
        jnp.bfloat16
    )
    upward_grad = (hidden_grad * swish).astype(jnp.bfloat16)
    gate_gradient = left_transposed(normed_mid, gate_grad)
    up_gradient = left_transposed(normed_mid, upward_grad)
    mid_partial = right_transposed(gate_grad, gate_weight) + right_transposed(
        upward_grad, up_weight
    )
    mid_grad = lax.psum_scatter(
        mid_partial.astype(jnp.bfloat16), "head", scatter_dimension=0, tiled=True
    ).astype(jnp.float32)
    middle_norm_grad, feed_gain_partial = norm_backward(middle, feed_gain, mid_grad)
    middle_grad = cotangent_rows.astype(jnp.float32) + middle_norm_grad
    attention_grad = middle_grad.astype(jnp.bfloat16)
    attention_grad_all = lax.all_gather(attention_grad, "head", axis=0, tiled=True)
    mixed_grad = right_transposed(attention_grad_all, out_proj).astype(jnp.bfloat16)
    proj_gradient = left_transposed(mixed, attention_grad_all)
    query_grad, key_grad, value_grad = attend_backward(
        queries,
        keys,
        values,
        segments,
        log_totals,
        mixed_grad.reshape(length, heads_here, head_width),
        block,
        scale,
    )
    query_pre_grad = (
        rotate(query_grad, cosine[:, None], -sine[:, None]).reshape(length, -1).astype(jnp.bfloat16)
    )
    query_up_gradient = left_transposed(latent_normed, query_pre_grad)
    latent_partial = right_transposed(query_pre_grad, query_up)
    latent_rows, key_rows, value_rows = (
        lax.psum_scatter(
            latent_partial.astype(jnp.bfloat16), "head", scatter_dimension=0, tiled=True
        ).astype(jnp.float32),
        lax.psum_scatter(
            key_grad.astype(jnp.bfloat16), "head", scatter_dimension=0, tiled=True
        ).astype(jnp.float32),
        lax.psum_scatter(
            value_grad.astype(jnp.bfloat16), "head", scatter_dimension=0, tiled=True
        ).astype(jnp.float32),
    )
    own_latent = lax.dynamic_slice_in_dim(latent, first_row, rows, 0)
    latent_grad_full, query_gain_partial = norm_backward(own_latent, query_gain, latent_rows)
    latent_grad = latent_grad_full.astype(jnp.bfloat16)
    own_cosine = lax.dynamic_slice_in_dim(cosine, first_row, rows, 0)
    own_sine = lax.dynamic_slice_in_dim(sine, first_row, rows, 0)
    key_pre_grad = rotate(key_rows, own_cosine, -own_sine).astype(jnp.bfloat16)
    value_low_grad = value_rows.astype(jnp.bfloat16)
    in_grad = (
        right_transposed(latent_grad, query_down)
        + right_transposed(key_pre_grad, key_proj)
        + right_transposed(value_low_grad, value_proj)
    )
    query_down_partial = left_transposed(normed_rows, latent_grad)
    key_proj_partial = left_transposed(normed_rows, key_pre_grad)
    value_proj_partial = left_transposed(normed_rows, value_low_grad)
    input_norm_grad, attention_gain_partial = norm_backward(rows_in, attention_gain, in_grad)
    input_gradient = middle_grad + input_norm_grad
    shared = lax.psum(
        (
            query_down_partial,
            key_proj_partial,
            value_proj_partial,
            attention_gain_partial,
            query_gain_partial,
            feed_gain_partial,
        ),
        ("tok", "head"),
    )
    local = (
        lax.psum(query_up_gradient.astype(jnp.bfloat16), "tok").astype(jnp.float32),
        lax.psum(proj_gradient.astype(jnp.bfloat16), "tok").astype(jnp.float32),
        lax.psum(gate_gradient.astype(jnp.bfloat16), "tok").astype(jnp.float32),
        lax.psum(up_gradient.astype(jnp.bfloat16), "tok").astype(jnp.float32),
        lax.psum(down_gradient.astype(jnp.bfloat16), "tok").astype(jnp.float32),
    )
    return (
        block_output[None],
        input_gradient[None],
        shared[3],
        shared[0],
        shared[4],
        local[0],
        shared[1],
        shared[2],
        local[1],
        shared[5],
        local[2],
        local[3],
        local[4],
    )


def solution(mesh):
    in_specs = (
        P("tok", "head", None),
        P("tok", None),
        P("tok", None),
        P(),
        P(),
        P(),
        P(None, "head"),
        P(),
        P(),
        P("head", None),
        P(),
        P(None, "head"),
        P(None, "head"),
        P("head", None),
        P("tok", "head", None),
    )
    out_specs = (
        P("tok", "head", None),
        P("tok", "head", None),
        P(),
        P(),
        P(),
        P(None, "head"),
        P(),
        P(),
        P("head", None),
        P(),
        P(None, "head"),
        P(None, "head"),
        P("head", None),
    )
    return jax.shard_map(body, mesh=mesh, in_specs=in_specs, out_specs=out_specs, check_vma=False)
```

profile of v0, /device:TPU:0, one launch (start us, length us, event | category | flops | bytes accessed | tf_op | source)
XLA Modules:
  0.0 1391.0 jit_solution(3441061401580680849)
XLA Ops:
  12.9 47.6 %all-gather.6.cloned.1.call-done = bf16[1536,2048]{1,0:T(8,128)(2,1)} async-done(((bf16[192,2048]{1,0:T(8,128)(2,1)}), bf16[1536,2048]{1,0:T(8,128)(2,1)}) %all-gather.6.cloned.1.call-update) | async-done | bytes 6291472 | tf_op jit(solution)/shard_map/all_gather | solution.py:156
  60.6 11.9 multiply_reduce_fusion
  87.4 5.1 fusion.90
  104.7 5.5 convolution_convert_fusion.7
  110.2 35.5 %while.28 = (s32[]{:T(128)}, bf16[3,512,2,256]{3,2,1,0:T(2,128)(2,1)}, f32[3,2,512]{2,1,0:T(2,128)}, s32[3]{0:T(128)S(1)}, s32[1,1536]{1,0:T(1,128)S(1)}, /*inde...) while((s32[]{:T(128)}, ...), condition=%wide.region_5.6_spmd.clone, body=%wide.region_2.5_spmd.clone.sunk | while | flops 1632108032 | bytes 28897524 | solution.py:86
  148.8 5.3 convolution_convert_fusion.1
  154.2 61.9 %reduce-scatter.9.cloned.1.call-done = bf16[192,2048]{1,0:T(8,128)(2,1)} async-done(((bf16[1536,2048]{1,0:T(8,128)(2,1)}), bf16[192,2048]{1,0:T(8,128)(2,1)}) %reduce-scatter.9.cloned.1.call-update) | async-done | bytes 786448 | tf_op jit(solution)/shard_map/reduce_scatter | solution.py:169
  220.9 45.0 %all-gather.8.cloned.1.call-done = bf16[1536,2048]{1,0:T(8,128)(2,1)} async-done(((bf16[192,2048]{1,0:T(8,128)(2,1)}), bf16[1536,2048]{1,0:T(8,128)(2,1)}) %all-gather.8.cloned.1.call-update) | async-done | bytes 6291472 | tf_op jit(solution)/shard_map/all_gather | solution.py:177
  266.0 10.5 fusion.98
  276.5 6.4 fusion.97
  282.9 30.6 %all-gather.12.cloned.1.call-done = bf16[1,1536,2048]{2,1,0:T(8,128)(2,1)} async-done(((bf16[1,192,2048]{2,1,0:T(8,128)(2,1)}), bf16[1,1536,2048]{2,1,0:T(8,128)(2,1)}) %all-gather.12.cloned.1.call-update) | async-done | bytes 6291472 | tf_op jit(solution)/shard_map/all_gather | solution.py:191
  313.4 11.9 multiply_convert_fusion.1
  325.4 5.1 fusion.99
  330.5 9.0 add_convert_fusion
  339.6 61.9 %reduce-scatter.13.cloned.1.call-done = bf16[192,2048]{1,0:T(8,128)(2,1)} async-done(((bf16[1536,2048]{1,0:T(8,128)(2,1)}), bf16[192,2048]{1,0:T(8,128)(2,1)}) %reduce-scatter.13.cloned.1.call-update) | async-done | bytes 786448 | tf_op jit(solution)/shard_map/reduce_scatter | solution.py:203
  407.2 45.6 %all-gather.10.cloned.1.call-done = bf16[1536,2048]{1,0:T(8,128)(2,1)} async-done(((bf16[192,2048]{1,0:T(8,128)(2,1)}), bf16[1536,2048]{1,0:T(8,128)(2,1)}) %all-gather.10.cloned.1.call-update) | async-done | bytes 6291472 | tf_op jit(solution)/shard_map/all_gather | solution.py:209
  452.8 8.0 convolution_convert_fusion.6
  461.3 70.3 %while.29 = (s32[]{:T(128)}, f32[1536,256]{1,0:T(8,128)}, f32[1536,256]{1,0:T(8,128)}, f32[3,512,2,256]{3,1,0,2:T(8,128)}, s32[3]{0:T(128)}, /*index=5*/s32[1,15...) while((s32[]{:T(128)}, f32[1536,256]{1,0:T(8,128)}, ...), condition=%wide.region_14.15_spmd.clone, body=%wide.region_12.14_spmd.clone.sunk | while | flops 4045274624 | bytes 101515776 | solution.py:122
  548.0 5.2 convolution_convert_fusion.2
  553.3 8.8 convolution_convert_fusion
  562.2 9.8 fusion.51
  572.0 9.1 convolution_convert_fusion.3
  581.2 5.9 convolution_convert_fusion.4
  601.7 8.7 reduce-scatter.17.cloned.1.call-done
  613.3 47.3 %reduce-scatter.15.cloned.1.call-done = bf16[192,1024]{1,0:T(8,128)(2,1)} async-done(((bf16[1536,1024]{1,0:T(8,128)(2,1)}), bf16[192,1024]{1,0:T(8,128)(2,1)}) %reduce-scatter.15.cloned.1.call-update) | async-done | bytes 393232 | tf_op jit(solution)/shard_map/reduce_scatter | solution.py:228
  662.1 6.3 fusion.91
  677.5 40.5 %all-reduce = (f32[2048]{0:T(1024)}, f32[1024]{0:T(1024)}, f32[2048]{0:T(1024)}) all-reduce(f32[2048]{0:T(1024)S(1)} %get-tuple-element.268, f32[1024]{0:T(1024)S(1)} %get-tuple-element.264, f32[2048]{0:T(1024)S(1)} %copy-done.34), channel_id=1, replica_groups=mesh['tok'=4,'head'=8] {'tok','head'}, use_global_device_ids=true, to_apply=%region_21.22 | all-reduce | flops 5120 | bytes 40960 | tf_op jit(solution)/shard_map/psum | solution.py:255
  718.0 8.4 reduce-scatter.11.cloned.1.call-done
  726.4 5.2 fusion.67
  731.6 402.6 %all-reduce.8.cloned.1.call-done = (bf16[1024,512]{1,0:T(8,128)(2,1)}, bf16[512,2048]{1,0:T(8,128)(2,1)}, bf16[2048,704]{0,1:T(8,128)(2,1)}, bf16[2048,704]{0,1:T(8,128)(2,1)}, bf16[704,2048]{1,0:T(8,128)(2,1)}) async-done(((bf16[1024,512]{1,0:T(8,128)(2,1)}, bf16[512,2048]{1,0:T(8,128)(2,1)}, bf16[2048,704]{0,1:T(8,128)(2,1)}, bf16[2048,704]{0,1:T(8,128)(2,1)}, bf16[704,2048]{1,0:T(8,128)(2,1)}), ...) | async-done | bytes 11796496 | tf_op jit(solution)/shard_map/psum | solution.py:267
  1150.0 221.6 %all-reduce.6.cloned.1.call-done = (f32[2048,1024]{1,0:T(8,128)}, f32[2048,256]{1,0:T(8,128)}, f32[2048,256]{1,0:T(8,128)}) async-done(((f32[2048,1024]{1,0:T(8,128)}, f32[2048,256]{1,0:T(8,128)}, f32[2048,256]{1,0:T(8,128)}), (f32[2048,1024]{1,0:T(8,128)}, f32[2048,256]{1,0:T(8,128)}, f32[2048,256]{1,0:T(8,128)})) %all-reduce.6.cloned.1.call-update) | async-done | bytes 12582928 | tf_op jit(solution)/shard_map/psum | solution.py:255
  1371.6 8.6 copy.124
  (311 shorter events, 206.0 us)
Async XLA Ops:
  7.2 306.3 %copy-start = (bf16[704,2048]{1,0:T(8,128)(2,1)S(1)}, bf16[704,2048]{1,0:T(8,128)(2,1)}, u32[]{:S(2)}) copy-start(bf16[704,2048]{1,0:T(8,128)(2,1)} %param.32) | copy-start | bytes 8650756
  7.2 53.4 %all-gather.6.cloned.1.call-start = ((), (), s32[]{:S(2)}) async-start(), calls=%async_computation.6 | async-start | bytes 7077888 | tf_op jit(solution)/shard_map/all_gather | solution.py:156
  12.2 203.8 %reduce-scatter.9.cloned.1.call-start = ((), (), s32[]{:S(2)}) async-start(), calls=%async_computation.7 | async-start | bytes 7077888 | tf_op jit(solution)/shard_map/reduce_scatter | solution.py:169
  60.6 11.9 copy-start.21
  60.6 11.9 copy-start.48
  72.5 14.9 %copy-start.35 = (f32[1536]{0:T(1024)}, f32[1536]{0:T(1024)S(1)}, u32[]{:S(2)}) copy-start(f32[1536]{0:T(1024)S(1)} %add_rsqrt_fusion) | copy-start | bytes 18436
  154.1 63.7 %copy-start.28 = (f32[2048]{0:T(1024)S(1)}, f32[2048]{0:T(1024)}, u32[]{:S(2)}) copy-start(f32[2048]{0:T(1024)} %param.29) | copy-start | bytes 24580
  154.1 111.9 %all-gather.8.cloned.1.call-start = ((), (), s32[]{:S(2)}) async-start(), calls=%async_computation.8 | async-start | bytes 7077888 | tf_op jit(solution)/shard_map/all_gather | solution.py:177
  217.7 186.7 %copy-start.37 = (f32[192]{0:T(256)}, f32[192]{0:T(256)S(1)}, u32[]{:S(2)}) copy-start(f32[192]{0:T(256)S(1)} %get-tuple-element.352) | copy-start | bytes 2308
  217.7 186.7 %copy-start.41 = (f32[192]{0:T(256)}, f32[192]{0:T(256)S(1)}, u32[]{:S(2)}) copy-start(f32[192]{0:T(256)S(1)} %get-tuple-element.351) | copy-start | bytes 2308
  220.3 93.1 %all-gather.12.cloned.1.call-start = ((), (), s32[]{:S(2)}) async-start(), calls=%async_computation.14 | async-start | bytes 7077888 | tf_op jit(solution)/shard_map/all_gather | solution.py:191
  220.9 180.6 %reduce-scatter.13.cloned.1.call-start = ((), (), s32[]{:S(2)}) async-start(), calls=%async_computation.10 | async-start | bytes 7077888 | tf_op jit(solution)/shard_map/reduce_scatter | solution.py:203
  266.0 10.5 copy-start.47
  266.0 10.5 copy-start.49
  313.4 11.9 copy-start.50
  339.6 113.2 %all-gather.10.cloned.1.call-start = ((), (), s32[]{:S(2)}) async-start(), calls=%async_computation.11 | async-start | bytes 7077888 | tf_op jit(solution)/shard_map/all_gather | solution.py:209
  407.2 189.4 %reduce-scatter.19.cloned.1.call-start = ((), (), s32[]{:S(2)}) async-start(), calls=%async_computation.15 | async-start | bytes 884736
  536.5 73.9 %reduce-scatter.17.cloned.1.call-start = ((), (), s32[]{:S(2)}) async-start(), calls=%async_computation.13 | async-start | bytes 884736 | tf_op jit(solution)/shard_map/reduce_scatter | solution.py:234
  541.2 119.4 %reduce-scatter.15.cloned.1.call-start = ((), (), s32[]{:S(2)}) async-start(), calls=%async_computation.12 | async-start | bytes 3538944 | tf_op jit(solution)/shard_map/reduce_scatter | solution.py:228
  553.2 173.2 %reduce-scatter.11.cloned.1.call-start = ((), (), s32[]{:S(2)}) async-start(), calls=%async_computation.9 | async-start | bytes 7077888 | tf_op jit(solution)/shard_map/reduce_scatter | solution.py:183
  562.1 572.0 %all-reduce.8.cloned.1.call-start = ((), (), s32[]{:S(2)}) async-start(), calls=%async_computation.17 | async-start | bytes 23592960 | tf_op jit(solution)/shard_map/psum | solution.py:267
  562.2 9.8 copy-start.55
  562.2 18.9 %slice-start.2 = ((s8[6291456]{0:T(1024)(128)(4,1)}), s8[4194304]{0:T(1024)(128)(4,1)S(1)}, s32[]{:S(2)}) async-start(s8[6291456]{0:T(1024)(128)(4,1)} %bitcast.210), calls=%async_computation.20 | async-start | bytes 8388608
  572.0 15.1 %slice-start = ((s8[6291456]{0:T(1024)(128)(4,1)}), s8[4194304]{0:T(1024)(128)(4,1)S(1)}, s32[]{:S(2)}) async-start(s8[6291456]{0:T(1024)(128)(4,1)} %bitcast.201), calls=%async_computation.18 | async-start | bytes 8388608
  572.0 18.4 %slice-start.4 = ((s8[6291456]{0:T(1024)(128)(4,1)}), s8[4194304]{0:T(1024)(128)(4,1)S(1)}, s32[]{:S(2)}) async-start(s8[6291456]{0:T(1024)(128)(4,1)} %bitcast.212), calls=%async_computation.22 | async-start | bytes 8388608
  581.2 9.2 slice-start.5
  595.2 776.4 %all-reduce.6.cloned.1.call-start = ((), (), s32[]{:S(2)}) async-start(), calls=%async_computation.16 | async-start | bytes 25165824 | tf_op jit(solution)/shard_map/psum | solution.py:255
  675.5 50.9 %copy-start.29 = (f32[2048]{0:T(1024)S(1)}, f32[2048]{0:T(1024)}, u32[]{:S(2)}) copy-start(f32[2048]{0:T(1024)} %param.29) | copy-start | bytes 24580
  675.5 50.9 %copy-start.38 = (f32[192]{0:T(256)S(1)}, f32[192]{0:T(256)}, u32[]{:S(2)}) copy-start(f32[192]{0:T(256)} %copy-done.37) | copy-start | bytes 2308
  675.5 50.8 %copy-start.42 = (f32[192]{0:T(256)S(1)}, f32[192]{0:T(256)}, u32[]{:S(2)}) copy-start(f32[192]{0:T(256)} %copy-done.41) | copy-start | bytes 2308
  675.6 50.8 %copy-start.44 = (f32[192]{0:T(256)S(1)}, f32[192]{0:T(256)}, u32[]{:S(2)}) copy-start(f32[192]{0:T(256)} %copy-done.43) | copy-start | bytes 2308
  675.6 50.8 %copy-start.46 = (f32[192]{0:T(256)S(1)}, f32[192]{0:T(256)}, u32[]{:S(2)}) copy-start(f32[192]{0:T(256)} %get-tuple-element.347) | copy-start | bytes 2308
  (58 other events, 190.6 us)
Sparse Core Ops, SparseCore 0:
  12.3 48.2 all-gather.5
  154.2 61.7 reduce-scatter.8
  220.4 45.4 all-gather.7
  267.9 45.5 all-gather.11
  339.7 61.7 reduce-scatter.12
  407.3 45.5 all-gather.9
  536.6 35.0 reduce-scatter.18
  575.4 34.9 reduce-scatter.16
  614.4 46.2 reduce-scatter.14
  664.2 62.1 reduce-scatter.10
  730.7 403.4 all-reduce.7
  1141.0 230.5 all-reduce.5
where the time goes:
time: 1400 us; the launch traced here: 1390 us
  waiting for transfers between devices  982 us (70%)
  matrix products  204 us (15%)
  other arithmetic  75.6 us (5%)
  local copies, waits for them, and re-layouts  62.4 us (4%)
  blocking collectives  40.5 us (3%)
  between operations  15 us (1%)
    psum x1, waiting for transfers between devices, body(): lax.psum(query_up_gradient.astype(jnp.bfloat16), 'tok').astype(jnp.float32)  403 us
    psum x1, waiting for transfers between devices, body(): lax.psum((query_down_partial, key_proj_partial, value_proj_partial, atten...  222 us
    reduce_scatter x1, waiting for transfers between devices, body(): lax.psum_scatter(mid_partial.astype(jnp.bfloat16), 'head', scatter_dimens...  61.9 us
    reduce_scatter x1, waiting for transfers between devices, body(): lax.psum_scatter(jnp.dot(mixed, out_proj, preferred_element_type=jnp.floa...  61.9 us
    all_gather x1, waiting for transfers between devices, body(): normed_in = lax.all_gather(normed_rows, 'head', axis=0, tiled=True)  47.6 us
    reduce_scatter x1, waiting for transfers between devices, body(): lax.psum_scatter(latent_partial.astype(jnp.bfloat16), 'head', scatter_dim...  47.3 us
    dot_general x8, matrix products, right_transposed(): lax.dot_general(left, right, (((1,), (1,)), ((), ())), preferred_element_...  46 us
    all_gather x1, waiting for transfers between devices, body(): lax.all_gather(attention_grad, 'head', axis=0, tiled=True)  45.6 us
  transfers between devices with their start and end apart: 12, of which 11 were waited for; matrix products, arithmetic and copies ran while one was open for 9% of the time, Pallas kernels for 0%

commit v1 on v0

--- a/solution.py
+++ b/solution.py
@@ -253,15 +253,18 @@
     input_norm_grad, attention_gain_partial = norm_backward(rows_in, attention_gain, in_grad)
     input_gradient = middle_grad + input_norm_grad
     shared = lax.psum(
-        (
-            query_down_partial,
-            key_proj_partial,
-            value_proj_partial,
-            attention_gain_partial,
-            query_gain_partial,
-            feed_gain_partial,
+        lax.psum(
+            (
+                query_down_partial,
+                key_proj_partial,
+                value_proj_partial,
+                attention_gain_partial,
+                query_gain_partial,
+                feed_gain_partial,
+            ),
+            "head",
         ),
-        ("tok", "head"),
+        "tok",
     )
     local = (
         lax.psum(query_up_gradient.astype(jnp.bfloat16), "tok").astype(jnp.float32),

time: 1400 us -> 1770 us (1.26)
  waiting for transfers between devices: 982 us -> 1350 us
    psum x0 -> x1, waiting for transfers between devices: none -> 413 us  [body(): lax.psum(lax.psum((query_down_partial, key_proj_partial, value_proj_parti...]
    psum x1, waiting for transfers between devices: 222 us -> 131 us  [body(): lax.psum((query_down_partial, key_proj_partial, value_proj_partial, atten...]
    reduce_scatter x1, waiting for transfers between devices: 8.7 us -> 33.6 us  [body(): lax.psum_scatter(value_grad.astype(jnp.bfloat16), 'head', scatter_dimensi...]
    psum x0 -> x1, blocking collectives: none -> 19.5 us  [body(): lax.psum(lax.psum((query_down_partial, key_proj_partial, value_proj_parti...]
  transfers between devices with their start and end apart: 12 -> 13, of which waited for: 11 -> 13; matrix products, arithmetic and copies ran while one was open for 9% -> 6% of each run, Pallas kernels for 0% -> 0%
where the time goes in v1:
time: 1770 us; the launch traced here: 1760 us
  waiting for transfers between devices  1350 us (76%)
  matrix products  204 us (12%)
  other arithmetic  75.7 us (4%)
  local copies, waits for them, and re-layouts  62.2 us (4%)
  blocking collectives  43 us (2%)
    psum x1, waiting for transfers between devices, body(): lax.psum(lax.psum((query_down_partial, key_proj_partial, value_proj_parti...  413 us
    psum x1, waiting for transfers between devices, body(): lax.psum(query_up_gradient.astype(jnp.bfloat16), 'tok').astype(jnp.float32)  403 us
    psum x1, waiting for transfers between devices, body(): lax.psum((query_down_partial, key_proj_partial, value_proj_partial, atten...  131 us
    reduce_scatter x1, waiting for transfers between devices, body(): lax.psum_scatter(jnp.dot(mixed, out_proj, preferred_element_type=jnp.floa...  61.8 us
    reduce_scatter x1, waiting for transfers between devices, body(): lax.psum_scatter(mid_partial.astype(jnp.bfloat16), 'head', scatter_dimens...  61.8 us
    all_gather x1, waiting for transfers between devices, body(): normed_in = lax.all_gather(normed_rows, 'head', axis=0, tiled=True)  47.6 us
    reduce_scatter x1, waiting for transfers between devices, body(): lax.psum_scatter(latent_partial.astype(jnp.bfloat16), 'head', scatter_dim...  47.3 us
    dot_general x8, matrix products, right_transposed(): lax.dot_general(left, right, (((1,), (1,)), ((), ())), preferred_element_...  45.8 us
  transfers between devices with their start and end apart: 13, of which 13 were waited for; matrix products, arithmetic and copies ran while one was open for 6% of the time, Pallas kernels for 0%

profile of v1, /device:TPU:0, one launch (start us, length us, event | category | flops | bytes accessed | tf_op | source)
XLA Modules:
  0.0 1763.4 jit_solution(7744799965044913285)
XLA Ops:
  13.0 47.6 %all-gather.6.cloned.1.call-done = bf16[1536,2048]{1,0:T(8,128)(2,1)} async-done(((bf16[192,2048]{1,0:T(8,128)(2,1)}), bf16[1536,2048]{1,0:T(8,128)(2,1)}) %all-gather.6.cloned.1.call-update) | async-done | bytes 6291472 | tf_op jit(solution)/shard_map/all_gather | solution.py:156
  60.6 11.9 multiply_reduce_fusion
  104.7 5.5 convolution_convert_fusion.7
  110.2 35.5 %while.28 = (s32[]{:T(128)}, bf16[3,512,2,256]{3,2,1,0:T(2,128)(2,1)}, f32[3,2,512]{2,1,0:T(2,128)}, s32[3]{0:T(128)S(1)}, s32[1,1536]{1,0:T(1,128)S(1)}, /*inde...) while((s32[]{:T(128)}, ...), condition=%wide.region_5.6_spmd.clone, body=%wide.region_2.5_spmd.clone.sunk | while | flops 1632108032 | bytes 28897524 | solution.py:86
  148.8 5.3 convolution_convert_fusion.1
  154.2 61.8 %reduce-scatter.9.cloned.1.call-done = bf16[192,2048]{1,0:T(8,128)(2,1)} async-done(((bf16[1536,2048]{1,0:T(8,128)(2,1)}), bf16[192,2048]{1,0:T(8,128)(2,1)}) %reduce-scatter.9.cloned.1.call-update) | async-done | bytes 786448 | tf_op jit(solution)/shard_map/reduce_scatter | solution.py:169
  221.0 45.0 %all-gather.8.cloned.1.call-done = bf16[1536,2048]{1,0:T(8,128)(2,1)} async-done(((bf16[192,2048]{1,0:T(8,128)(2,1)}), bf16[1536,2048]{1,0:T(8,128)(2,1)}) %all-gather.8.cloned.1.call-update) | async-done | bytes 6291472 | tf_op jit(solution)/shard_map/all_gather | solution.py:177
  266.0 10.5 fusion.98
  276.5 6.4 fusion.97
  282.9 30.5 %all-gather.12.cloned.1.call-done = bf16[1,1536,2048]{2,1,0:T(8,128)(2,1)} async-done(((bf16[1,192,2048]{2,1,0:T(8,128)(2,1)}), bf16[1,1536,2048]{2,1,0:T(8,128)(2,1)}) %all-gather.12.cloned.1.call-update) | async-done | bytes 6291472 | tf_op jit(solution)/shard_map/all_gather | solution.py:191
  313.5 12.0 multiply_convert_fusion.1
  330.6 9.0 add_convert_fusion
  339.6 61.8 %reduce-scatter.13.cloned.1.call-done = bf16[192,2048]{1,0:T(8,128)(2,1)} async-done(((bf16[1536,2048]{1,0:T(8,128)(2,1)}), bf16[192,2048]{1,0:T(8,128)(2,1)}) %reduce-scatter.13.cloned.1.call-update) | async-done | bytes 786448 | tf_op jit(solution)/shard_map/reduce_scatter | solution.py:203
  407.2 45.6 %all-gather.10.cloned.1.call-done = bf16[1536,2048]{1,0:T(8,128)(2,1)} async-done(((bf16[192,2048]{1,0:T(8,128)(2,1)}), bf16[1536,2048]{1,0:T(8,128)(2,1)}) %all-gather.10.cloned.1.call-update) | async-done | bytes 6291472 | tf_op jit(solution)/shard_map/all_gather | solution.py:209
  452.8 8.0 convolution_convert_fusion.6
  461.3 70.3 %while.29 = (s32[]{:T(128)}, f32[1536,256]{1,0:T(8,128)}, f32[1536,256]{1,0:T(8,128)}, f32[3,512,2,256]{3,1,0,2:T(8,128)}, s32[3]{0:T(128)}, /*index=5*/s32[1,15...) while((s32[]{:T(128)}, f32[1536,256]{1,0:T(8,128)}, ...), condition=%wide.region_14.15_spmd.clone, body=%wide.region_12.14_spmd.clone.sunk | while | flops 4045274624 | bytes 101515776 | solution.py:122
  548.0 5.2 convolution_convert_fusion.2
  554.7 16.9 reduce-scatter.19.cloned.1.call-done
  576.8 33.6 %reduce-scatter.17.cloned.1.call-done = bf16[192,256]{1,0:T(8,128)(2,1)} async-done(((bf16[1536,256]{1,0:T(8,128)(2,1)}), bf16[192,256]{1,0:T(8,128)(2,1)}) %reduce-scatter.17.cloned.1.call-update) | async-done | bytes 98320 | tf_op jit(solution)/shard_map/reduce_scatter | solution.py:234
  613.3 47.3 %reduce-scatter.15.cloned.1.call-done = bf16[192,1024]{1,0:T(8,128)(2,1)} async-done(((bf16[1536,1024]{1,0:T(8,128)(2,1)}), bf16[192,1024]{1,0:T(8,128)(2,1)}) %reduce-scatter.15.cloned.1.call-update) | async-done | bytes 393232 | tf_op jit(solution)/shard_map/reduce_scatter | solution.py:228
  662.1 6.3 fusion.91
  668.6 8.7 convolution_convert_fusion
  677.3 9.9 fusion.51
  687.3 9.3 convolution_convert_fusion.3
  696.6 5.9 convolution_convert_fusion.4
  710.8 130.9 %all-reduce.9.cloned.1.call-done = (f32[2048,1024]{1,0:T(8,128)}, f32[2048,256]{1,0:T(8,128)}, f32[2048,256]{1,0:T(8,128)}) async-done(((f32[2048,1024]{1,0:T(8,128)}, f32[2048,256]{1,0:T(8,128)}, f32[2048,256]{1,0:T(8,128)}), (f32[2048,1024]{1,0:T(8,128)}, f32[2048,256]{1,0:T(8,128)}, f32[2048,256]{1,0:T(8,128)})) %all-reduce.9.cloned.1.call-update) | async-done | bytes 12582928 | tf_op jit(solution)/shard_map/psum | solution.py:256
  850.2 23.5 %all-reduce = (f32[2048]{0:T(1024)S(1)}, f32[1024]{0:T(1024)S(1)}, f32[2048]{0:T(1024)S(1)}) all-reduce(f32[2048]{0:T(1024)S(1)} %get-tuple-element.268, f32[1024]{0:T(1024)S(1)} %get-tuple-element.264, f32[2048]{0:T(1024)S(1)} %copy-done.34), channel_id=1, replica_groups=mesh['tok'=4,'head'=8] {'head'}, use_global_device_ids=true, to_apply=%region_21.22 | all-reduce | flops 5120 | bytes 40960 | tf_op jit(solution)/shard_map/psum | solution.py:256
  873.7 19.5 %all-reduce.2 = (f32[2048]{0:T(1024)}, f32[1024]{0:T(1024)}, f32[2048]{0:T(1024)}) all-reduce(f32[2048]{0:T(1024)S(1)} %get-tuple-element.312, f32[1024]{0:T(1024)S(1)} %get-tuple-element.313, f32[2048]{0:T(1024)S(1)} %get-tuple-element.314), channel_id=1, replica_groups=mesh['tok'=4,'head'=8] {'tok'}, use_global_device_ids=true, to_apply=%region_22.23 | all-reduce | flops 5120 | bytes 40960 | tf_op jit(solution)/shard_map/psum | solution.py:255
  893.2 13.8 reduce-scatter.11.cloned.1.call-done
  912.2 402.7 %all-reduce.13.cloned.1.call-done = (bf16[1024,512]{1,0:T(8,128)(2,1)}, bf16[512,2048]{1,0:T(8,128)(2,1)}, bf16[2048,704]{0,1:T(8,128)(2,1)}, bf16[2048,704]{0,1:T(8,128)(2,1)}, bf16[704,2048]{1,0:T(8,128)(2,1)}) async-done(((bf16[1024,512]{1,0:T(8,128)(2,1)}, bf16[512,2048]{1,0:T(8,128)(2,1)}, bf16[2048,704]{0,1:T(8,128)(2,1)}, bf16[2048,704]{0,1:T(8,128)(2,1)}, bf16[704,2048]{1,0:T(8,128)(2,1)}), ...) | async-done | bytes 11796496 | tf_op jit(solution)/shard_map/psum | solution.py:270
  1330.9 413.5 %all-reduce.11.cloned.1.call-done = (f32[2048,1024]{1,0:T(8,128)}, f32[2048,256]{1,0:T(8,128)}, f32[2048,256]{1,0:T(8,128)}) async-done(((f32[2048,1024]{1,0:T(8,128)}, f32[2048,256]{1,0:T(8,128)}, f32[2048,256]{1,0:T(8,128)}), (f32[2048,1024]{1,0:T(8,128)}, f32[2048,256]{1,0:T(8,128)}, f32[2048,256]{1,0:T(8,128)})) %all-reduce.11.cloned.1.call-update) | async-done | bytes 12582928 | tf_op jit(solution)/shard_map/psum | solution.py:255
  1744.4 8.6 copy.127
  (315 shorter events, 221.4 us)
Async XLA Ops:
  7.2 306.3 %copy-start = (bf16[704,2048]{1,0:T(8,128)(2,1)S(1)}, bf16[704,2048]{1,0:T(8,128)(2,1)}, u32[]{:S(2)}) copy-start(bf16[704,2048]{1,0:T(8,128)(2,1)} %param.32) | copy-start | bytes 8650756
  7.2 53.4 %all-gather.6.cloned.1.call-start = ((), (), s32[]{:S(2)}) async-start(), calls=%async_computation.6 | async-start | bytes 7077888 | tf_op jit(solution)/shard_map/all_gather | solution.py:156
  12.2 203.8 %reduce-scatter.9.cloned.1.call-start = ((), (), s32[]{:S(2)}) async-start(), calls=%async_computation.7 | async-start | bytes 7077888 | tf_op jit(solution)/shard_map/reduce_scatter | solution.py:169
  60.6 11.9 copy-start.21
  60.6 11.9 copy-start.48
  72.5 14.9 copy-start.35
  154.1 63.7 %copy-start.28 = (f32[2048]{0:T(1024)S(1)}, f32[2048]{0:T(1024)}, u32[]{:S(2)}) copy-start(f32[2048]{0:T(1024)} %param.29) | copy-start | bytes 24580
  154.1 111.9 %all-gather.8.cloned.1.call-start = ((), (), s32[]{:S(2)}) async-start(), calls=%async_computation.8 | async-start | bytes 7077888 | tf_op jit(solution)/shard_map/all_gather | solution.py:177
  217.7 186.7 %copy-start.37 = (f32[192]{0:T(256)}, f32[192]{0:T(256)S(1)}, u32[]{:S(2)}) copy-start(f32[192]{0:T(256)S(1)} %get-tuple-element.358) | copy-start | bytes 2308
  217.7 186.7 %copy-start.41 = (f32[192]{0:T(256)}, f32[192]{0:T(256)S(1)}, u32[]{:S(2)}) copy-start(f32[192]{0:T(256)S(1)} %get-tuple-element.357) | copy-start | bytes 2308
  220.3 93.1 %all-gather.12.cloned.1.call-start = ((), (), s32[]{:S(2)}) async-start(), calls=%async_computation.14 | async-start | bytes 7077888 | tf_op jit(solution)/shard_map/all_gather | solution.py:191
  220.9 180.6 %reduce-scatter.13.cloned.1.call-start = ((), (), s32[]{:S(2)}) async-start(), calls=%async_computation.10 | async-start | bytes 7077888 | tf_op jit(solution)/shard_map/reduce_scatter | solution.py:203
  266.0 10.5 copy-start.47
  266.0 10.5 copy-start.49
  313.5 12.0 copy-start.50
  339.6 113.2 %all-gather.10.cloned.1.call-start = ((), (), s32[]{:S(2)}) async-start(), calls=%async_computation.11 | async-start | bytes 7077888 | tf_op jit(solution)/shard_map/all_gather | solution.py:209
  407.2 164.5 %reduce-scatter.19.cloned.1.call-start = ((), (), s32[]{:S(2)}) async-start(), calls=%async_computation.15 | async-start | bytes 884736
  536.5 73.9 %reduce-scatter.17.cloned.1.call-start = ((), (), s32[]{:S(2)}) async-start(), calls=%async_computation.13 | async-start | bytes 884736 | tf_op jit(solution)/shard_map/reduce_scatter | solution.py:234
  541.2 119.4 %reduce-scatter.15.cloned.1.call-start = ((), (), s32[]{:S(2)}) async-start(), calls=%async_computation.12 | async-start | bytes 3538944 | tf_op jit(solution)/shard_map/reduce_scatter | solution.py:228
  553.2 288.5 %all-reduce.9.cloned.1.call-start = ((), (), s32[]{:S(2)}) async-start(), calls=%async_computation.16 | async-start | bytes 25165824 | tf_op jit(solution)/shard_map/psum | solution.py:256
  576.8 83.8 %copy-start.33 = (f32[1024]{0:T(1024)S(1)}, f32[1024]{0:T(1024)}, u32[]{:S(2)}) copy-start(f32[1024]{0:T(1024)} %param.24) | copy-start | bytes 12292
  668.5 238.5 %reduce-scatter.11.cloned.1.call-start = ((), (), s32[]{:S(2)}) async-start(), calls=%async_computation.9 | async-start | bytes 7077888 | tf_op jit(solution)/shard_map/reduce_scatter | solution.py:183
  677.3 637.7 %all-reduce.13.cloned.1.call-start = ((), (), s32[]{:S(2)}) async-start(), calls=%async_computation.18 | async-start | bytes 23592960 | tf_op jit(solution)/shard_map/psum | solution.py:270
  677.3 19.2 %slice-start.2 = ((s8[6291456]{0:T(1024)(128)(4,1)}), s8[4194304]{0:T(1024)(128)(4,1)S(1)}, s32[]{:S(2)}) async-start(s8[6291456]{0:T(1024)(128)(4,1)} %bitcast.210), calls=%async_computation.21 | async-start | bytes 8388608
  687.3 15.3 slice-start
  687.3 18.5 %slice-start.4 = ((s8[6291456]{0:T(1024)(128)(4,1)}), s8[4194304]{0:T(1024)(128)(4,1)S(1)}, s32[]{:S(2)}) async-start(s8[6291456]{0:T(1024)(128)(4,1)} %bitcast.212), calls=%async_computation.23 | async-start | bytes 8388608
  710.5 1033.9 %all-reduce.11.cloned.1.call-start = ((), (), s32[]{:S(2)}) async-start(), calls=%async_computation.17 | async-start | bytes 25165824 | tf_op jit(solution)/shard_map/psum | solution.py:255
  848.3 58.7 %copy-start.29 = (f32[2048]{0:T(1024)S(1)}, f32[2048]{0:T(1024)}, u32[]{:S(2)}) copy-start(f32[2048]{0:T(1024)} %param.29) | copy-start | bytes 24580
  848.3 58.7 %copy-start.38 = (f32[192]{0:T(256)S(1)}, f32[192]{0:T(256)}, u32[]{:S(2)}) copy-start(f32[192]{0:T(256)} %copy-done.37) | copy-start | bytes 2308
  848.3 58.7 %copy-start.42 = (f32[192]{0:T(256)S(1)}, f32[192]{0:T(256)}, u32[]{:S(2)}) copy-start(f32[192]{0:T(256)} %copy-done.41) | copy-start | bytes 2308
  848.3 58.7 %copy-start.44 = (f32[192]{0:T(256)S(1)}, f32[192]{0:T(256)}, u32[]{:S(2)}) copy-start(f32[192]{0:T(256)} %copy-done.43) | copy-start | bytes 2308
  848.3 58.7 %copy-start.46 = (f32[192]{0:T(256)S(1)}, f32[192]{0:T(256)}, u32[]{:S(2)}) copy-start(f32[192]{0:T(256)} %get-tuple-element.353) | copy-start | bytes 2308
  (59 other events, 202.8 us)
Sparse Core Ops, SparseCore 0:
  12.4 48.2 all-gather.5
  154.2 61.7 reduce-scatter.8
  220.4 45.4 all-gather.7
  267.9 45.5 all-gather.11
  339.7 61.7 reduce-scatter.12
  407.3 45.4 all-gather.9
  536.6 35.0 reduce-scatter.18
  575.4 34.9 reduce-scatter.16
  614.3 46.2 reduce-scatter.14
  668.6 173.0 all-reduce.8
  845.1 61.8 reduce-scatter.10
  911.4 403.4 all-reduce.12
  1318.0 426.3 all-reduce.10
